TPU v7x, 512 devices: a whole 4x4x16 slice. The times are simulated.
512 devices in a mesh: rep: 16 (over x, z_lo), mp: 32 (over z_hi, y, core).
Axes of the slice: x: 4, y: 4, z: 16 (z_hi: 4, z_lo: 4; z = z_hi * 4 + z_lo), core: 2. Of those that a mesh axis runs over, the one named last changes fastest.
Arguments:
- dense_feats: bfloat16 [65536, 13], P(('rep', 'mp')), may hold values from -6 to 6
- bag_counts: int32 [65536, 32, 64], P('rep', 'mp'), may hold values from 0 to 2
- emb_rows: bfloat16 [32, 64, 256], P('mp'), may hold values from -0.625 to 0.625
- v_emb: bfloat16 [8192, 256], P('mp'), may hold values from -0.0625 to 0.0625
- u_emb: bfloat16 [256, 8192], P(None, 'mp'), may hold values from -0.375 to 0.375
- b_emb: bfloat16 [8192], P('mp'), may hold values from -3 to 3
- v_bot: bfloat16 [256, 256], replicated, may hold values from -0.375 to 0.375
- u_bot: bfloat16 [256, 256], replicated, may hold values from -0.375 to 0.375
- b_bot: bfloat16 [256], replicated, may hold values from -3 to 3
- w_first: bfloat16 [13, 1024], replicated, may hold values from -1.75 to 1.75
- b_first: bfloat16 [1024], replicated, may hold values from -3 to 3
- w_second: bfloat16 [1024, 256], replicated, may hold values from -0.1875 to 0.1875
- b_second: bfloat16 [256], replicated, may hold values from -3 to 3
- cot_cross: bfloat16 [65536, 8192], P(('rep', 'mp')), may hold values from -24 to 24
- cot_bottom: bfloat16 [65536, 256], P(('rep', 'mp')), may hold values from -6 to 6
Outputs:
- cross_emb: bfloat16 [65536, 8192], P(('rep', 'mp'))
- cross_bot: bfloat16 [65536, 256], P(('rep', 'mp'))
- grad_table: bfloat16 [32, 64, 256], P('mp')
- grad_v_emb: bfloat16 [8192, 256], P('mp')
- grad_u_emb: bfloat16 [256, 8192], P(None, 'mp')
- grad_b_emb: bfloat16 [8192], P('mp')
- grad_v_bot: bfloat16 [256, 256], replicated
- grad_u_bot: bfloat16 [256, 256], replicated
- grad_b_bot: bfloat16 [256], replicated
- grad_w_first: bfloat16 [13, 1024], replicated
- grad_b_first: bfloat16 [1024], replicated
- grad_w_second: bfloat16 [1024, 256], replicated
- grad_b_second: bfloat16 [256], replicated
Inputs may be any that keep to these rules, and one draw needn't show every extreme that they name: bag_counts[s, t, j] is how often row j of table t occurs in the bag of sample s.
All inputs are finite; a program needn't handle non-finite values.
Results may differ from a plain program's by a relative error of at most 0.029.
Values may be sent and summed in bfloat16 or wider, within the bound.
A program may use at most 64 MiB of HBM per device.

v0:
```python
import math
import jax
import jax.numpy as jnp
from jax import lax
from jax.sharding import PartitionSpec as P


def silu_slope(inputs):
    gate_value = jax.nn.sigmoid(inputs)
    return gate_value * (1.0 + inputs * (1.0 - gate_value))


def contract_rows(left_side, right_side):
    return lax.dot_general(
        left_side, right_side, (((0,), (0,)), ((), ())), preferred_element_type=jnp.float32
    )


def contract_cols(left_side, right_side):
    return lax.dot_general(
        left_side, right_side, (((1,), (1,)), ((), ())), preferred_element_type=jnp.float32
    )


def local(
    dense_feats,
    bag_counts,
    emb_rows,
    v_emb,
    u_emb,
    b_emb,
    v_bot,
    u_bot,
    b_bot,
    w_first,
    b_first,
    w_second,
    b_second,
    cot_cross,
    cot_bottom,
):
    group_size = lax.axis_size("mp")
    own_rows = dense_feats.shape[0]
    first_row = lax.axis_index("mp") * own_rows
    grad_scale = 1.0 / math.sqrt(own_rows * group_size * lax.axis_size("rep"))
    counts = bag_counts[:, 0, :].astype(jnp.bfloat16)
    pooled = jnp.dot(counts, emb_rows[0], preferred_element_type=jnp.float32).astype(jnp.bfloat16)
    partial_value = jnp.dot(pooled, v_emb, preferred_element_type=jnp.float32)
    first_pre = jnp.dot(dense_feats, w_first, preferred_element_type=jnp.float32) + b_first.astype(
        jnp.float32
    )
    first_act = jax.nn.silu(first_pre).astype(jnp.bfloat16)
    second_pre = jnp.dot(first_act, w_second, preferred_element_type=jnp.float32) + b_second.astype(
        jnp.float32
    )
    bottom = jax.nn.silu(second_pre).astype(jnp.bfloat16)
    own_part = lax.dynamic_slice_in_dim(partial_value, first_row, own_rows, 0) + jnp.dot(
        bottom, v_bot, preferred_element_type=jnp.float32
    )
    partial_value = lax.dynamic_update_slice_in_dim(partial_value, own_part, first_row, 0)
    low_rank = lax.psum(partial_value.astype(jnp.bfloat16), "mp")
    lift_emb = jnp.dot(low_rank, u_emb, preferred_element_type=jnp.float32) + b_emb.astype(
        jnp.float32
    )
    pooled_full = pooled.astype(jnp.float32)
    cross_local = (pooled_full * (lift_emb + 1.0)).astype(jnp.bfloat16)
    cross_emb = lax.all_to_all(cross_local, "mp", split_axis=0, concat_axis=1, tiled=True)
    own_low = lax.dynamic_slice_in_dim(low_rank, first_row, own_rows, 0)
    lift_bottom = jnp.dot(own_low, u_bot, preferred_element_type=jnp.float32) + b_bot.astype(
        jnp.float32
    )
    bottom_full = bottom.astype(jnp.float32)
    cross_bot = (bottom_full * (lift_bottom + 1.0)).astype(jnp.bfloat16)
    cot_rows = lax.all_to_all(cot_cross, "mp", split_axis=1, concat_axis=0, tiled=True).astype(
        jnp.float32
    )
    d_lift = cot_rows * pooled_full
    d_lift_round = d_lift.astype(jnp.bfloat16)
    own_back = lax.psum_scatter(
        contract_cols(d_lift_round, u_emb).astype(jnp.bfloat16),
        "mp",
        scatter_dimension=0,
        tiled=True,
    ).astype(jnp.float32)
    cot_low = cot_bottom.astype(jnp.float32)
    d_bottom_lift = cot_low * bottom_full
    d_bottom_round = d_bottom_lift.astype(jnp.bfloat16)
    own_d_low = (own_back + contract_cols(d_bottom_round, u_bot)).astype(jnp.bfloat16)
    d_low = lax.all_gather(own_d_low, "mp", axis=0, tiled=True)
    d_pooled = (cot_rows * (lift_emb + 1.0) + contract_cols(d_low, v_emb)).astype(jnp.bfloat16)
    grad_table = grad_scale * contract_rows(counts, d_pooled)
    grad_v = grad_scale * contract_rows(pooled, d_low)
    grad_u = grad_scale * contract_rows(low_rank, d_lift_round)
    grad_b = grad_scale * jnp.sum(d_lift, axis=0)
    d_bottom = cot_low * (lift_bottom + 1.0) + contract_cols(own_d_low, v_bot)
    grad_vb = grad_scale * contract_rows(bottom, own_d_low)
    grad_ub = grad_scale * contract_rows(own_low, d_bottom_round)
    grad_bb = grad_scale * jnp.sum(d_bottom_lift, axis=0)
    d_second = d_bottom * silu_slope(second_pre)
    d_second_round = d_second.astype(jnp.bfloat16)
    grad_ws = grad_scale * contract_rows(first_act, d_second_round)
    grad_bs = grad_scale * jnp.sum(d_second, axis=0)
    d_first = contract_cols(d_second_round, w_second) * silu_slope(first_pre)
    d_first_round = d_first.astype(jnp.bfloat16)
    grad_wf = grad_scale * contract_rows(dense_feats, d_first_round)
    grad_bf = grad_scale * jnp.sum(d_first, axis=0)
    dense_sums = lax.psum(
        (grad_wf, grad_bf, grad_ws, grad_bs, grad_vb, grad_ub, grad_bb), ("rep", "mp")
    )
    table_sums = (
        lax.psum(grad_table.astype(jnp.bfloat16), "rep").astype(jnp.float32),
        lax.psum(grad_v.astype(jnp.bfloat16), "rep").astype(jnp.float32),
        lax.psum(grad_u.astype(jnp.bfloat16), "rep").astype(jnp.float32),
        lax.psum(grad_b.astype(jnp.bfloat16), "rep").astype(jnp.float32),
    )
    return (
        cross_emb,
        cross_bot,
        table_sums[0][None].astype(jnp.bfloat16),
        table_sums[1].astype(jnp.bfloat16),
        table_sums[2].astype(jnp.bfloat16),
        table_sums[3].astype(jnp.bfloat16),
        dense_sums[4].astype(jnp.bfloat16),
        dense_sums[5].astype(jnp.bfloat16),
        dense_sums[6].astype(jnp.bfloat16),
        dense_sums[0].astype(jnp.bfloat16),
        dense_sums[1].astype(jnp.bfloat16),
        dense_sums[2].astype(jnp.bfloat16),
        dense_sums[3].astype(jnp.bfloat16),
    )


def solution(mesh):
    return jax.shard_map(
        local,
        mesh=mesh,
        in_specs=(
            P(("rep", "mp"), None),
            P("rep", "mp", None),
            P("mp", None, None),
            P("mp", None),
            P(None, "mp"),
            P("mp"),
            P(),
            P(),
            P(),
            P(),
            P(),
            P(),
            P(),
            P(("rep", "mp"), None),
            P(("rep", "mp"), None),
        ),
        out_specs=(
            P(("rep", "mp"), None),
            P(("rep", "mp"), None),
            P("mp", None, None),
            P("mp", None),
            P(None, "mp"),
            P("mp"),
            P(),
            P(),
            P(),
            P(),
            P(),
            P(),
            P(),
        ),
        check_vma=False,
    )
```

profile of v0, /device:TPU:8, one launch (start us, length us, event | category | flops | bytes accessed | tf_op | source)
XLA Modules:
  0.0 923.8 jit_solution(9754976400988497330)
XLA Ops:
  7.2 0.0 copy-start
  7.2 3.2 copy.33
  10.4 0.0 copy-start.8
  10.4 18.5 %all-to-all-start.1 = ((bf16[128,32,256]{2,0,1:T(8,128)(2,1)}), bf16[128,32,256]{2,0,1:T(8,128)(2,1)}, u32[]{:S(2)}, u32[]{:S(2)}) async-start(bf16[128,32,256]{2,0,1:T(8,128)(2,1)} %bitcast.58), calls=%async_computation.1 | async-start | bytes 4194304 | tf_op jit(solution)/shard_map/all_to_all | solution.py:74
  29.0 0.0 copy-start.11
  29.0 0.0 all-reduce.7.cloned.1.call-start
  29.1 0.3 convolution_add_fusion.2
  29.4 0.0 copy-start.5
  29.4 0.8 copy-done.5
  30.2 1.0 fusion.22
  31.1 2.0 convolution_convert_fusion.1
  33.1 0.7 fusion.35
  33.9 0.2 copy-done.9
  34.0 0.2 fusion.8
  34.2 1.5 convert_element_type.134
  35.8 0.0 all-reduce.7.cloned.1.call-update
  35.8 0.0 reduce-scatter.2.cloned.1.call-start
  35.8 0.6 copy-done.16
  36.4 399.7 %all-reduce.7.cloned.1.call-done = bf16[4096,256]{1,0:T(8,128)(2,1)} async-done(((bf16[4096,256]{1,0:T(8,128)(2,1)}), bf16[4096,256]{1,0:T(8,128)(2,1)}) %all-reduce.7.cloned.1.call-update) | async-done | bytes 2097168 | tf_op jit(solution)/shard_map/psum | solution.py:61
  436.1 6.4 bitcast_multiply_fusion
  442.6 1.3 copy-done.1
  443.9 2.1 convolution_convert_fusion
  446.0 0.0 reduce-scatter.2.cloned.1.call-update
  446.1 0.0 copy-start.17
  446.1 21.6 %all-to-all-start = ((bf16[32,128,256]{2,1,0:T(8,128)(2,1)}), bf16[32,128,256]{2,1,0:T(8,128)(2,1)}, u32[]{:S(2)}, u32[]{:S(2)}) async-start(bf16[32,128,256]{2,1,0:T(8,128)(2,1)} %bitcast.59), calls=%async_computation | async-start | bytes 4194304 | tf_op jit(solution)/shard_map/all_to_all | solution.py:67
  467.7 0.0 all-gather.2.cloned.1.call-start
  467.7 151.9 %reduce-scatter.2.cloned.1.call-done = bf16[128,256]{1,0:T(8,128)(2,1)} async-done(((bf16[4096,256]{1,0:T(8,128)(2,1)}), bf16[128,256]{1,0:T(8,128)(2,1)}) %reduce-scatter.2.cloned.1.call-update) | async-done | bytes 65552 | tf_op jit(solution)/shard_map/reduce_scatter | solution.py:79
  619.7 1.7 fusion.11
  621.3 0.0 all-gather.2.cloned.1.call-update
  621.4 0.0 all-reduce.9.cloned.1.call-start
  621.4 1.1 convolution_multiply_fusion.2
  622.5 1.6 fusion.21
  624.2 0.0 copy-start.18
  624.2 3.7 fusion.7
  627.9 0.2 convolution_multiply_fusion.3
  628.1 0.2 fusion.34
  628.4 0.4 fusion.33
  628.7 0.2 fusion.13
  628.9 1.4 convolution_multiply_fusion
  630.3 114.5 %all-reduce.10 = (bf16[256,256]{1,0:T(8,128)(2,1)}, bf16[256,256]{1,0:T(8,128)(2,1)}, bf16[256]{0:T(256)(128)(2,1)}, bf16[13,1024]{1,0:T(8,128)(2,1)}, bf16[1024...) all-reduce(f32[256,256]{1,0:T(8,128)S(1)} %convolution_multiply_fus, ...), channel_id=1, replica_groups=mesh['rep'=16,'mp'=32] {'rep','mp'}, use_global_device_ids=true, to_apply=%region_7.8 | all-reduce | flops 408064 | bytes 2448384 | tf_op jit(solution)/shard_map/psum | solution.py:107
  744.8 3.0 fusion.6
  747.8 0.0 all-reduce.9.cloned.1.call-update
  747.8 4.5 fusion.15
  752.3 78.6 %all-reduce.1 = (bf16[1,64,256]{2,1,0:T(8,128)(2,1)}, bf16[256]{0:T(256)(128)(2,1)}) all-reduce(bf16[1,64,256]{2,1,0:T(8,128)(2,1)S(1)} %fusion.15, bf16[256]{0:T(256)(128)(2,1)S(1)} %multiply_convert_fusion.2), channel_id=1, replica_groups=mesh['rep'=16,'mp'=32] {'rep'}, use_global_device_ids=true, to_apply=%region_2.3 | all-reduce | flops 16640 | bytes 66560 | tf_op jit(solution)/shard_map/psum | solution.py:111
  830.9 3.1 copy.31
  834.0 80.1 %all-reduce.9.cloned.1.call-done = (bf16[256,256]{1,0:T(8,128)(2,1)}, bf16[256,256]{1,0:T(8,128)(2,1)}) async-done(((bf16[256,256]{1,0:T(8,128)(2,1)}, bf16[256,256]{1,0:T(8,128)(2,1)}), (bf16[256,256]{1,0:T(8,128)(2,1)}, bf16[256,256]{1,0:T(8,128)(2,1)})) %all-reduce.9.cloned.1.call-update) | async-done | bytes 262160 | tf_op jit(solution)/shard_map/psum | solution.py:112
  914.1 1.6 copy.52
  915.7 1.6 copy.53
  (39 shorter events, 0.1 us)
Async XLA Ops:
  7.2 23.0 %copy-start = (bf16[1024,256]{1,0:T(8,128)(2,1)S(1)}, bf16[1024,256]{1,0:T(8,128)(2,1)}, u32[]{:S(2)}) copy-start(bf16[1024,256]{1,0:T(8,128)(2,1)} %param.26) | copy-start | bytes 1572868
  10.4 18.6 %copy-start.15 = (bf16[256]{0:T(256)(128)(2,1)S(1)}, bf16[256]{0:T(256)(128)(2,1)}, u32[]{:S(2)}) copy-start(bf16[256]{0:T(256)(128)(2,1)} %param.27) | copy-start | bytes 1540
  10.4 18.6 %copy-start.14 = (bf16[1024]{0:T(1024)(128)(2,1)S(1)}, bf16[1024]{0:T(1024)(128)(2,1)}, u32[]{:S(2)}) copy-start(bf16[1024]{0:T(1024)(128)(2,1)} %param.25) | copy-start | bytes 6148
  10.4 18.7 %copy-start.12 = (bf16[13,1024]{1,0:T(8,128)(2,1)S(1)}, bf16[13,1024]{1,0:T(8,128)(2,1)}, u32[]{:S(2)}) copy-start(bf16[13,1024]{1,0:T(8,128)(2,1)} %param.24) | copy-start | bytes 79876
  10.4 18.7 %copy-start.13 = (bf16[128,13]{0,1:T(8,128)(2,1)S(1)}, bf16[128,13]{0,1:T(8,128)(2,1)}, u32[]{:S(2)}) copy-start(bf16[128,13]{0,1:T(8,128)(2,1)} %param.15) | copy-start | bytes 9988
  10.4 19.7 %copy-start.8 = (bf16[128,256]{1,0:T(8,128)(2,1)S(1)}, bf16[128,256]{1,0:T(8,128)(2,1)}, u32[]{:S(2)}) copy-start(bf16[128,256]{1,0:T(8,128)(2,1)} %param.29) | copy-start | bytes 196612
  10.4 425.7 %all-to-all-start.1 = ((bf16[128,32,256]{2,0,1:T(8,128)(2,1)}), bf16[128,32,256]{2,0,1:T(8,128)(2,1)}, u32[]{:S(2)}, u32[]{:S(2)}) async-start(bf16[128,32,256]{2,0,1:T(8,128)(2,1)} %bitcast.58), calls=%async_computation.1 | async-start | bytes 4194304 | tf_op jit(solution)/shard_map/all_to_all | solution.py:74
  29.0 2.1 copy-start.11
  29.0 407.2 %all-reduce.7.cloned.1.call-start = ((), (), s32[]{:S(2)}) async-start(), calls=%async_computation.3 | async-start | bytes 4194304 | tf_op jit(solution)/shard_map/psum | solution.py:61
  29.4 0.8 copy-start.5
  31.1 2.0 copy-start.4
  33.1 0.9 copy-start.9
  35.8 0.7 copy-start.16
  35.8 400.4 %copy-start.3 = (bf16[256,256]{1,0:T(8,128)(2,1)S(1)}, bf16[256,256]{1,0:T(8,128)(2,1)}, u32[]{:S(2)}) copy-start(bf16[256,256]{1,0:T(8,128)(2,1)} %param.19) | copy-start | bytes 393220
  35.8 583.9 %reduce-scatter.2.cloned.1.call-start = ((), (), s32[]{:S(2)}) async-start(), calls=%async_computation.4 | async-start | bytes 2162688 | tf_op jit(solution)/shard_map/reduce_scatter | solution.py:79
  442.6 1.3 copy-start.1
  446.0 173.6 %copy-start.7 = (bf16[256,256]{1,0:T(8,128)(2,1)S(1)}, bf16[256,256]{1,0:T(8,128)(2,1)}, u32[]{:S(2)}) copy-start(bf16[256,256]{1,0:T(8,128)(2,1)} %param.22) | copy-start | bytes 393220
  446.1 175.3 %copy-start.17 = (bf16[256]{0:T(256)(128)(2,1)S(1)}, bf16[256]{0:T(256)(128)(2,1)}, u32[]{:S(2)}) copy-start(bf16[256]{0:T(256)(128)(2,1)} %param.23) | copy-start | bytes 1540
  446.1 384.9 %all-to-all-start = ((bf16[32,128,256]{2,1,0:T(8,128)(2,1)}), bf16[32,128,256]{2,1,0:T(8,128)(2,1)}, u32[]{:S(2)}, u32[]{:S(2)}) async-start(bf16[32,128,256]{2,1,0:T(8,128)(2,1)} %bitcast.59), calls=%async_computation | async-start | bytes 4194304 | tf_op jit(solution)/shard_map/all_to_all | solution.py:67
  467.7 277.1 %all-gather.2.cloned.1.call-start = ((), (), s32[]{:S(2)}) async-start(), calls=%async_computation.5 | async-start | bytes 2162688 | tf_op jit(solution)/shard_map/all_gather | solution.py:89
  621.4 292.8 %all-reduce.9.cloned.1.call-start = ((), (), s32[]{:S(2)}) async-start(), calls=%async_computation.6 | async-start | bytes 524288 | tf_op jit(solution)/shard_map/psum | solution.py:112
  624.2 3.7 copy-start.2
  624.2 4.0 copy-start.10
  624.2 4.0 copy-start.18
  624.2 4.2 copy-start.6
Sparse Core Ops, SparseCore 0:
  35.9 400.1 all-reduce.6
  446.2 173.4 reduce-scatter.1
  623.8 74.0 all-gather.1
  747.9 166.1 all-reduce.8
where the time goes:
time: 924 us
  waiting for transfers between devices  632 us (68%)
  blocking collectives  193 us (21%)
  starting transfers between devices  40.3 us (4%)
  matrix products  30.5 us (3%)
  between operations  14.1 us (2%)
  local copies, waits for them, and re-layouts  12.5 us (1%)
    psum x1, waiting for transfers between devices, local(): low_rank = lax.psum(partial_value.astype(jnp.bfloat16), 'mp')  400 us
    reduce_scatter x1, waiting for transfers between devices, local(): lax.psum_scatter(contract_cols(d_lift_round, u_emb).astype(jnp.bfloat16),...  152 us
    psum x1, blocking collectives, local(): lax.psum((grad_wf, grad_bf, grad_ws, grad_bs, grad_vb, grad_ub, grad_bb),...  115 us
    psum x1, waiting for transfers between devices, local(): lax.psum(grad_v.astype(jnp.bfloat16), 'rep').astype(jnp.float32)  80.1 us
    psum x1, blocking collectives, local(): lax.psum(grad_table.astype(jnp.bfloat16), 'rep').astype(jnp.float32)  78.6 us
    all_to_all x1, starting transfers between devices, local(): lax.all_to_all(cross_local, 'mp', split_axis=0, concat_axis=1, tiled=True)  21.6 us
    all_to_all x1, starting transfers between devices, local(): lax.all_to_all(cot_cross, 'mp', split_axis=1, concat_axis=0, tiled=True)  18.5 us
  transfers between devices with their start and end apart: 6, of which 3 were waited for; matrix products, arithmetic and copies ran while one was open for 3% of the time, Pallas kernels for 0%

commit v1 on v0

--- a/solution.py
+++ b/solution.py
@@ -104,9 +104,11 @@
     d_first_round = d_first.astype(jnp.bfloat16)
     grad_wf = grad_scale * contract_rows(dense_feats, d_first_round)
     grad_bf = grad_scale * jnp.sum(d_first, axis=0)
-    dense_sums = lax.psum(
-        (grad_wf, grad_bf, grad_ws, grad_bs, grad_vb, grad_ub, grad_bb), ("rep", "mp")
-    )
+
+    def mix_the_seats_all(tile_in):
+        return lax.psum(lax.psum(tile_in, axis_name="mp"), axis_name="rep")
+
+    dense_sums = mix_the_seats_all((grad_wf, grad_bf, grad_ws, grad_bs, grad_vb, grad_ub, grad_bb))
     table_sums = (
         lax.psum(grad_table.astype(jnp.bfloat16), "rep").astype(jnp.float32),
         lax.psum(grad_v.astype(jnp.bfloat16), "rep").astype(jnp.float32),

time: 924 us -> 1280 us (1.39)
  waiting for transfers between devices: 632 us -> 815 us
  blocking collectives: 193 us -> 360 us
    psum x0 -> x1, waiting for transfers between devices: none -> 174 us  [mix_the_seats_all(): return lax.psum(lax.psum(tile_in, axis_name='mp'), axis_name='rep')]
    psum x1 -> x2, blocking collectives: 115 us -> 282 us  [mix_the_seats_all(): return lax.psum(lax.psum(tile_in, axis_name='mp'), axis_name='rep')]
  transfers between devices with their start and end apart: 6 -> 7, of which waited for: 3 -> 4; matrix products, arithmetic and copies ran while one was open for 3% -> 2% of each run, Pallas kernels for 0% -> 0%
where the time goes in v1:
time: 1280 us
  waiting for transfers between devices  815 us (64%)
  blocking collectives  360 us (28%)
  starting transfers between devices  40.3 us (3%)
  matrix products  32.3 us (3%)
  between operations  14 us (1%)
    psum x1, waiting for transfers between devices, local(): low_rank = lax.psum(partial_value.astype(jnp.bfloat16), 'mp')  402 us
    psum x2, blocking collectives, mix_the_seats_all(): return lax.psum(lax.psum(tile_in, axis_name='mp'), axis_name='rep')  282 us
    psum x1, waiting for transfers between devices, mix_the_seats_all(): return lax.psum(lax.psum(tile_in, axis_name='mp'), axis_name='rep')  174 us
    reduce_scatter x1, waiting for transfers between devices, local(): lax.psum_scatter(contract_cols(d_lift_round, u_emb).astype(jnp.bfloat16),...  149 us
    psum x1, waiting for transfers between devices, local(): lax.psum(grad_v.astype(jnp.bfloat16), 'rep').astype(jnp.float32)  90 us
    psum x1, blocking collectives, local(): lax.psum(grad_table.astype(jnp.bfloat16), 'rep').astype(jnp.float32)  78.1 us
  transfers between devices with their start and end apart: 7, of which 4 were waited for; matrix products, arithmetic and copies ran while one was open for 2% of the time, Pallas kernels for 0%

profile of v1, /device:TPU:8, one launch (start us, length us, event | category | flops | bytes accessed | tf_op | source)
XLA Modules:
  0.0 1275.1 jit_solution(11124720484701194761)
XLA Ops:
  7.2 0.0 copy-start
  7.2 3.2 copy.33
  10.4 18.5 %all-to-all-start.1 = ((bf16[128,32,256]{2,0,1:T(8,128)(2,1)}), bf16[128,32,256]{2,0,1:T(8,128)(2,1)}, u32[]{:S(2)}, u32[]{:S(2)}) async-start(bf16[128,32,256]{2,0,1:T(8,128)(2,1)} %bitcast.58), calls=%async_computation.1 | async-start | bytes 4194304 | tf_op jit(solution)/shard_map/all_to_all | solution.py:74
  29.0 0.0 copy-start.8
  29.0 0.0 all-reduce.10.cloned.1.call-start
  29.1 0.2 convolution_add_fusion.2
  29.4 0.9 fusion.22
  30.3 2.0 convolution_convert_fusion.1
  32.4 0.7 fusion.35
  33.1 0.2 copy-done.7
  33.3 0.2 fusion.8
  33.4 1.5 convert_element_type.134
  35.0 0.0 all-reduce.10.cloned.1.call-update
  35.0 0.0 reduce-scatter.2.cloned.1.call-start
  35.0 0.6 copy-done.13
  35.6 402.2 %all-reduce.10.cloned.1.call-done = bf16[4096,256]{1,0:T(8,128)(2,1)} async-done(((bf16[4096,256]{1,0:T(8,128)(2,1)}), bf16[4096,256]{1,0:T(8,128)(2,1)}) %all-reduce.10.cloned.1.call-update) | async-done | bytes 2097168 | tf_op jit(solution)/shard_map/psum | solution.py:61
  437.8 6.4 bitcast_multiply_fusion
  444.3 1.4 copy-done.1
  445.6 2.1 convolution_convert_fusion
  447.7 0.0 reduce-scatter.2.cloned.1.call-update
  447.7 0.0 copy-start.14
  447.8 21.6 %all-to-all-start = ((bf16[32,128,256]{2,1,0:T(8,128)(2,1)}), bf16[32,128,256]{2,1,0:T(8,128)(2,1)}, u32[]{:S(2)}, u32[]{:S(2)}) async-start(bf16[32,128,256]{2,1,0:T(8,128)(2,1)} %bitcast.59), calls=%async_computation | async-start | bytes 4194304 | tf_op jit(solution)/shard_map/all_to_all | solution.py:67
  469.4 0.0 all-reduce.12.cloned.1.call-start
  469.4 1.8 convolution_multiply_fusion.2
  471.2 1.7 fusion.21
  472.9 148.6 %reduce-scatter.2.cloned.1.call-done = bf16[128,256]{1,0:T(8,128)(2,1)} async-done(((bf16[4096,256]{1,0:T(8,128)(2,1)}), bf16[128,256]{1,0:T(8,128)(2,1)}) %reduce-scatter.2.cloned.1.call-update) | async-done | bytes 65552 | tf_op jit(solution)/shard_map/reduce_scatter | solution.py:79
  621.5 1.1 fusion.11
  622.6 0.9 convolution_multiply_fusion.3
  623.5 1.3 fusion.34
  624.8 1.3 convolution_multiply_fusion
  626.1 0.0 all-reduce.12.cloned.1.call-update
  626.2 0.0 all-gather.2.cloned.1.call-start
  626.2 0.5 all-gather.2.cloned.1.call-update
  626.7 0.0 all-reduce.14.cloned.1.call-start
  626.8 3.6 fusion.7
  630.4 0.4 fusion.33
  630.8 0.2 fusion.13
  631.0 165.3 %all-reduce = (f32[256]{0:T(256)S(1)}, f32[13,1024]{1,0:T(8,128)S(1)}, f32[1024]{0:T(1024)S(1)}, f32[256]{0:T(256)S(1)}) all-reduce(f32[256]{0:T(256)S(1)} %broadcast_multiply_fusion.2, f32[13,1024]{1,0:T(8,128)S(1)} %fusion.13, f32[1024]{0:T(1024)S(1)} %broadcast_multiply_fusion, ...), channel_id=1, replica_groups=mesh['rep'=16,'mp'=32] {'mp'}, use_global_device_ids=true, to_apply=%region_12.13 | all-reduce | flops 14848 | bytes 118784 | tf_op jit(solution)/shard_map/psum | solution.py:109
  796.2 173.8 %all-reduce.12.cloned.1.call-done = (f32[256,256]{1,0:T(8,128)}, f32[256,256]{1,0:T(8,128)}, f32[1024,256]{1,0:T(8,128)}) async-done(((f32[256,256]{1,0:T(8,128)}, f32[256,256]{1,0:T(8,128)}, f32[1024,256]{1,0:T(8,128)}), (f32[256,256]{1,0:T(8,128)}, f32[256,256]{1,0:T(8,128)}, f32[1024,256]{1,0:T(8,128)})) %all-reduce.12.cloned.1.call-update) | async-done | bytes 1572880 | tf_op jit(solution)/shard_map/psum | solution.py:109
  970.0 116.6 %all-reduce.15 = (bf16[256,256]{1,0:T(8,128)(2,1)}, bf16[256,256]{1,0:T(8,128)(2,1)}, bf16[256]{0:T(256)(128)(2,1)}, bf16[13,1024]{1,0:T(8,128)(2,1)}, bf16[1024...) all-reduce(f32[256,256]{1,0:T(8,128)} %get-tuple-element.17, ...), channel_id=1, replica_groups=mesh['rep'=16,'mp'=32] {'rep'}, use_global_device_ids=true, to_apply=%region_8.9 | all-reduce | flops 408064 | bytes 2448384 | tf_op jit(solution)/shard_map/psum | solution.py:109
  1086.6 3.0 fusion.6
  1089.6 0.0 all-reduce.14.cloned.1.call-update
  1089.6 4.5 fusion.15
  1094.1 78.1 %all-reduce.3 = (bf16[1,64,256]{2,1,0:T(8,128)(2,1)}, bf16[256]{0:T(256)(128)(2,1)}) all-reduce(bf16[1,64,256]{2,1,0:T(8,128)(2,1)S(1)} %fusion.15, bf16[256]{0:T(256)(128)(2,1)S(1)} %multiply_convert_fusion.2), channel_id=1, replica_groups=mesh['rep'=16,'mp'=32] {'rep'}, use_global_device_ids=true, to_apply=%region_2.3 | all-reduce | flops 16640 | bytes 66560 | tf_op jit(solution)/shard_map/psum | solution.py:113
  1172.2 3.1 copy.31
  1175.4 90.0 %all-reduce.14.cloned.1.call-done = (bf16[256,256]{1,0:T(8,128)(2,1)}, bf16[256,256]{1,0:T(8,128)(2,1)}) async-done(((bf16[256,256]{1,0:T(8,128)(2,1)}, bf16[256,256]{1,0:T(8,128)(2,1)}), (bf16[256,256]{1,0:T(8,128)(2,1)}, bf16[256,256]{1,0:T(8,128)(2,1)})) %all-reduce.14.cloned.1.call-update) | async-done | bytes 262160 | tf_op jit(solution)/shard_map/psum | solution.py:114
  1265.4 1.6 copy.55
  1267.0 1.6 copy.56
  (35 shorter events, 0.1 us)
Async XLA Ops:
  7.2 22.2 %copy-start = (bf16[1024,256]{1,0:T(8,128)(2,1)S(1)}, bf16[1024,256]{1,0:T(8,128)(2,1)}, u32[]{:S(2)}) copy-start(bf16[1024,256]{1,0:T(8,128)(2,1)} %param.26) | copy-start | bytes 1572868
  10.4 18.6 %copy-start.12 = (bf16[256]{0:T(256)(128)(2,1)S(1)}, bf16[256]{0:T(256)(128)(2,1)}, u32[]{:S(2)}) copy-start(bf16[256]{0:T(256)(128)(2,1)} %param.27) | copy-start | bytes 1540
  10.4 18.6 %copy-start.11 = (bf16[1024]{0:T(1024)(128)(2,1)S(1)}, bf16[1024]{0:T(1024)(128)(2,1)}, u32[]{:S(2)}) copy-start(bf16[1024]{0:T(1024)(128)(2,1)} %param.25) | copy-start | bytes 6148
  10.4 18.7 %copy-start.9 = (bf16[13,1024]{1,0:T(8,128)(2,1)S(1)}, bf16[13,1024]{1,0:T(8,128)(2,1)}, u32[]{:S(2)}) copy-start(bf16[13,1024]{1,0:T(8,128)(2,1)} %param.24) | copy-start | bytes 79876
  10.4 18.7 %copy-start.10 = (bf16[128,13]{0,1:T(8,128)(2,1)S(1)}, bf16[128,13]{0,1:T(8,128)(2,1)}, u32[]{:S(2)}) copy-start(bf16[128,13]{0,1:T(8,128)(2,1)} %param.15) | copy-start | bytes 9988
  10.4 18.9 %copy-start.6 = (bf16[128,256]{1,0:T(8,128)(2,1)S(1)}, bf16[128,256]{1,0:T(8,128)(2,1)}, u32[]{:S(2)}) copy-start(bf16[128,256]{1,0:T(8,128)(2,1)} %param.29) | copy-start | bytes 196612
  10.4 427.4 %all-to-all-start.1 = ((bf16[128,32,256]{2,0,1:T(8,128)(2,1)}), bf16[128,32,256]{2,0,1:T(8,128)(2,1)}, u32[]{:S(2)}, u32[]{:S(2)}) async-start(bf16[128,32,256]{2,0,1:T(8,128)(2,1)} %bitcast.58), calls=%async_computation.1 | async-start | bytes 4194304 | tf_op jit(solution)/shard_map/all_to_all | solution.py:74
  29.0 1.4 copy-start.8
  29.0 408.8 %all-reduce.10.cloned.1.call-start = ((), (), s32[]{:S(2)}) async-start(), calls=%async_computation.3 | async-start | bytes 4194304 | tf_op jit(solution)/shard_map/psum | solution.py:61
  30.3 2.0 copy-start.4
  32.4 0.9 copy-start.7
  35.0 0.7 copy-start.13
  35.0 402.9 %copy-start.3 = (bf16[256,256]{1,0:T(8,128)(2,1)S(1)}, bf16[256,256]{1,0:T(8,128)(2,1)}, u32[]{:S(2)}) copy-start(bf16[256,256]{1,0:T(8,128)(2,1)} %param.19) | copy-start | bytes 393220
  35.0 586.5 %reduce-scatter.2.cloned.1.call-start = ((), (), s32[]{:S(2)}) async-start(), calls=%async_computation.4 | async-start | bytes 2162688 | tf_op jit(solution)/shard_map/reduce_scatter | solution.py:79
  444.3 1.4 copy-start.1
  447.7 21.7 %copy-start.14 = (bf16[256]{0:T(256)(128)(2,1)S(1)}, bf16[256]{0:T(256)(128)(2,1)}, u32[]{:S(2)}) copy-start(bf16[256]{0:T(256)(128)(2,1)} %param.23) | copy-start | bytes 1540
  447.7 23.5 %copy-start.5 = (bf16[256,256]{1,0:T(8,128)(2,1)S(1)}, bf16[256,256]{1,0:T(8,128)(2,1)}, u32[]{:S(2)}) copy-start(bf16[256,256]{1,0:T(8,128)(2,1)} %param.22) | copy-start | bytes 393220
  447.8 724.5 %all-to-all-start = ((bf16[32,128,256]{2,1,0:T(8,128)(2,1)}), bf16[32,128,256]{2,1,0:T(8,128)(2,1)}, u32[]{:S(2)}, u32[]{:S(2)}) async-start(bf16[32,128,256]{2,1,0:T(8,128)(2,1)} %bitcast.59), calls=%async_computation | async-start | bytes 4194304 | tf_op jit(solution)/shard_map/all_to_all | solution.py:67
  469.4 500.7 %all-reduce.12.cloned.1.call-start = ((), (), s32[]{:S(2)}) async-start(), calls=%async_computation.6 | async-start | bytes 3145728 | tf_op jit(solution)/shard_map/psum | solution.py:109
  622.6 3.6 copy-start.2
  626.2 460.5 %all-gather.2.cloned.1.call-start = ((), (), s32[]{:S(2)}) async-start(), calls=%async_computation.5 | async-start | bytes 2162688 | tf_op jit(solution)/shard_map/all_gather | solution.py:89
  626.7 638.7 %all-reduce.14.cloned.1.call-start = ((), (), s32[]{:S(2)}) async-start(), calls=%async_computation.7 | async-start | bytes 524288 | tf_op jit(solution)/shard_map/psum | solution.py:114
Sparse Core Ops, SparseCore 0:
  35.1 402.6 all-reduce.9
  447.8 173.5 reduce-scatter.1
  626.3 343.7 all-reduce.11
  973.6 87.4 all-gather.1
  1089.8 175.5 all-reduce.13
